TPU v7x, 256 devices: a whole 4x4x8 slice. The times are simulated.
256 devices in a mesh: dp: 2 (over core), ctx: 16 (over z_hi, y), exp: 8 (over x, z_lo).
Axes of the slice: x: 4, y: 4, z: 8 (z_hi: 4, z_lo: 2; z = z_hi * 2 + z_lo), core: 2. Of those that a mesh axis runs over, the one named last changes fastest.
Arguments:
- tokens: bfloat16 [2, 2048, 2560], P('dp', 'ctx'), may hold values from -6 to 6
- queries: bfloat16 [2, 2048, 16, 576], P('dp', 'ctx', 'exp'), may hold values from -240 to 240
- kv_weight: bfloat16 [2560, 576], P('exp'), may hold values from -0.125 to 0.125
- kv_gain: bfloat16 [512], replicated, may hold values from 0.5 to 1.5
- uv_weight: bfloat16 [16, 512, 128], P('exp'), may hold values from -0.75 to 0.75
- out_weight: bfloat16 [2048, 2560], P('exp'), may hold values from -0.5 to 0.5
- post_gain: bfloat16 [2560], replicated, may hold values from 0.5 to 1.5
- router_weight: bfloat16 [2560, 32], replicated, may hold values from -0.125 to 0.125
- expert_ids: int32 [2, 2048, 6], P('dp', 'ctx'), may hold values from 0 to 31, all different within a row; in each aligned block of 128 rows (0 to 127, 128 to 255, ..., all dimensions but the last counted through in order) at most 32 rows name the same one
- doc_ids: int32 [2, 2048], P('dp', 'ctx'), may hold values from 0 to 3, never falling along the last dimension, each value on 1 to 1024 neighbouring positions
- gate_weight: bfloat16 [32, 2560, 1536], P('ctx', None, 'exp'), may hold values from -0.125 to 0.125
- up_weight: bfloat16 [32, 2560, 1536], P('ctx', None, 'exp'), may hold values from -0.125 to 0.125
- down_weight: bfloat16 [32, 1536, 2560], P('ctx', 'exp'), may hold values from -0.15625 to 0.15625
- cotangent: bfloat16 [2, 2048, 2560], P('dp', 'ctx'), may hold values from -6 to 6
Outputs:
- layer_out: bfloat16 [2, 2048, 2560], P('dp', 'ctx')
- router_grad: float32 [2560, 32], replicated
- gate_grad: bfloat16 [32, 2560, 1536], P('ctx', 'dp', 'exp')
- up_grad: bfloat16 [32, 2560, 1536], P('ctx', 'dp', 'exp')
- down_grad: bfloat16 [32, 1536, 2560], P('ctx', 'exp', 'dp')
Inputs may be any that keep to these rules, and one draw needn't show every extreme that they name: `expert_ids`: in each aligned block of 128 positions of a sequence no expert is named by more than 32 of the block's assignments; the experts of one token differ. `doc_ids`: document numbers never fall along a sequence; a document has at most 1024 positions.
All inputs are finite; a program needn't handle non-finite values.
Results may differ from a plain program's by a relative error of at most 0.023.
The roundings to bfloat16 on the way count: a program that leaves them out, or rounds other values in their place, can miss the bound.
Values may be sent and summed in bfloat16 or wider, within the bound.
No kernel may reach another device: no remote copies, remote signals or barrier semaphores. Data moves between devices by JAX's collectives and lax.ppermute only.
A program may use at most 128 MiB of HBM per device.

v0:
```python
import jax
import jax.numpy as jnp
from jax import lax
from jax.sharding import PartitionSpec as P

ROPE = 64
NOPE = 128


epsilon = 1e-06


def from_everyone(array, axis):
    count = lax.axis_size(axis)
    return lax.all_to_all(
        jnp.broadcast_to(array[None], (count, *array.shape)), axis, 0, 0, tiled=True
    )


def taken_together(array, axis):
    everything = from_everyone(array, axis)
    return jnp.sum(everything, axis=0)


def in_one_piece(arrays, axis, split_dim, concat_dim, along):
    both = jnp.concatenate(arrays, axis=along)
    result, at, gathered = (
        lax.all_to_all(both, axis, split_axis=split_dim, concat_axis=concat_dim, tiled=True),
        0,
        [],
    )
    for a in arrays:
        gathered.append(lax.slice_in_dim(result, at, at + a.shape[along], axis=along))
        at += a.shape[along]
    return tuple(gathered)


def rms_scale(values, gain):
    return values * lax.rsqrt(jnp.mean(values * values, axis=-1, keepdims=True) + epsilon) * gain


def rotate(rope_part, positions):
    half_width = rope_part.shape[-1] // 2
    frequency = jnp.power(
        10000.0, -2.0 * jnp.arange(half_width, dtype=jnp.float32) / rope_part.shape[-1]
    )
    angles = positions.astype(jnp.float32)[:, None] * frequency[None, :]
    cosine = jnp.cos(angles)
    sine_part = jnp.sin(angles)
    first_half = rope_part[:, :half_width]
    second = rope_part[:, half_width:]
    return jnp.concatenate(
        [first_half * cosine - second * sine_part, second * cosine + first_half * sine_part], axis=1
    )


def route_slots(outgoing):
    moved = lax.all_to_all(outgoing, ("dp", "ctx"), split_axis=0, concat_axis=0, tiled=True)
    return moved


def local(
    tokens,
    queries,
    kv_weight,
    kv_gain,
    uv_weight,
    out_weight,
    post_gain,
    router_weight,
    expert_ids,
    doc_ids,
    gate_weight,
    up_weight,
    down_weight,
    cotangent,
):
    local_rows = tokens[0]
    seq_rows = local_rows.shape[0]
    model_width = local_rows.shape[1]
    latent_width = kv_gain.shape[0]
    row_share = kv_weight.shape[0]
    columns = lax.dynamic_slice_in_dim(local_rows, lax.axis_index("exp") * row_share, row_share, 1)
    compressed = taken_together(
        jnp.dot(columns, kv_weight, preferred_element_type=jnp.float32), "exp"
    )
    positions = lax.axis_index("ctx") * seq_rows + jnp.arange(seq_rows, dtype=jnp.int32)
    latent = rms_scale(compressed[:, :latent_width], kv_gain.astype(jnp.float32)).astype(
        jnp.bfloat16
    )
    rope_key = rotate(compressed[:, latent_width:], positions).astype(jnp.bfloat16)
    key_rows = jnp.concatenate([latent, rope_key], axis=1)
    all_keys, all_docs = (
        lax.all_gather(key_rows, "ctx", axis=0, tiled=True),
        lax.all_gather(doc_ids[0], "ctx", axis=0, tiled=True),
    )
    key_positions = jnp.arange(all_keys.shape[0], dtype=jnp.int32)
    allowed = (key_positions[None, :] <= positions[:, None]) & (
        all_docs[None, :] == doc_ids[0][:, None]
    )
    allowed = allowed[:, None, :]
    score_scale = (NOPE + ROPE) ** (-0.5)
    scores = (
        jnp.einsum("qhd,kd->qhk", queries[0], all_keys, preferred_element_type=jnp.float32)
        * score_scale
    )
    score_peak = jnp.max(jnp.where(allowed, scores, -1e30), axis=-1, keepdims=True)
    weights = jnp.exp(jnp.where(allowed, scores - score_peak, -1e30))
    weight_total = jnp.sum(weights, axis=-1, keepdims=True)
    mixed_latent = (
        jnp.einsum(
            "qhk,kl->qhl",
            weights.astype(jnp.bfloat16),
            all_keys[:, :latent_width],
            preferred_element_type=jnp.float32,
        )
        / weight_total
    )
    mixed_latent = mixed_latent.astype(jnp.bfloat16)
    head_values = (
        jnp.einsum("qhl,hlv->qhv", mixed_latent, uv_weight, preferred_element_type=jnp.float32)
        .astype(jnp.bfloat16)
        .reshape(seq_rows, -1)
    )
    head_part = jnp.dot(head_values, out_weight, preferred_element_type=jnp.float32)
    attention = lax.psum(head_part, "exp")
    hidden = (local_rows.astype(jnp.float32) + attention).astype(jnp.bfloat16)
    normed = rms_scale(hidden.astype(jnp.float32), post_gain.astype(jnp.float32)).astype(
        jnp.bfloat16
    )
    logits = jnp.dot(normed, router_weight, preferred_element_type=jnp.float32)
    router_probs = jax.nn.softmax(logits, axis=-1)
    picked_ids = expert_ids[0]
    experts_all = router_weight.shape[1]
    top_count = picked_ids.shape[1]
    chosen = jnp.take_along_axis(router_probs, picked_ids, axis=1)
    chosen_sum = jnp.sum(chosen, axis=1, keepdims=True)
    route_w = chosen / chosen_sum
    route_wb = route_w.astype(jnp.bfloat16)
    ctx_count = lax.axis_size("ctx")
    held_experts = experts_all // ctx_count
    capacity = (4 * seq_rows * top_count + 3 * experts_all - 1) // (3 * experts_all)
    flat_ids = picked_ids.reshape(-1)
    onehot = (flat_ids[:, None] == jnp.arange(experts_all, dtype=jnp.int32)[None, :]).astype(
        jnp.int32
    )
    slot_rank = jnp.sum((jnp.cumsum(onehot, axis=0) - onehot) * onehot, axis=1).reshape(
        seq_rows, top_count
    )
    dp_count = lax.axis_size("dp")
    local_count = held_experts // dp_count
    first_local = lax.axis_index("dp") * local_count
    gate_local = lax.dynamic_slice_in_dim(gate_weight, first_local, local_count, 0)
    up_local = lax.dynamic_slice_in_dim(up_weight, first_local, local_count, 0)
    down_local = lax.dynamic_slice_in_dim(down_weight, first_local, local_count, 0)
    home_ctx = picked_ids // held_experts
    remainder = picked_ids % held_experts
    home_dp = remainder // local_count
    within = remainder % local_count
    slot_index = ((home_dp * ctx_count + home_ctx) * local_count + within) * capacity + slot_rank
    slot_hits = (
        slot_index[:, :, None] == jnp.arange(experts_all * capacity, dtype=jnp.int32)[None, None, :]
    )
    dispatch = jnp.any(slot_hits, axis=1).astype(jnp.bfloat16)
    combine = jnp.sum(
        jnp.where(slot_hits, route_wb[:, :, None], jnp.zeros((), jnp.bfloat16)), axis=1
    )
    outgoing = jnp.einsum("se,sd->ed", dispatch, normed, preferred_element_type=jnp.float32).astype(
        jnp.bfloat16
    )
    outgoing = outgoing.reshape(-1, local_count, capacity, model_width)
    arrived = route_slots(outgoing)
    gate_pre = jnp.einsum("sjcd,jdf->sjcf", arrived, gate_local, preferred_element_type=jnp.float32)
    up_pre = jnp.einsum("sjcd,jdf->sjcf", arrived, up_local, preferred_element_type=jnp.float32)
    activated = (jax.nn.silu(gate_pre) * up_pre).astype(jnp.bfloat16)
    expert_part = jnp.einsum(
        "sjcf,jfd->sjcd", activated, down_local, preferred_element_type=jnp.float32
    ).astype(jnp.bfloat16)
    returned = lax.all_to_all(expert_part, ("dp", "ctx"), split_axis=0, concat_axis=0, tiled=True)
    returned = returned.reshape(experts_all * capacity, model_width)
    moe_part = jnp.dot(combine, returned, preferred_element_type=jnp.float32)
    cot_rows = cotangent[0]
    cross_terms = jnp.einsum("sd,ed->se", cot_rows, returned, preferred_element_type=jnp.float32)
    dweight_part = jnp.take_along_axis(cross_terms, slot_index, axis=1)
    moe, dweight = lax.psum((moe_part, dweight_part), "exp")
    layer_out = (hidden.astype(jnp.float32) + moe).astype(jnp.bfloat16)
    mean_term = jnp.sum(dweight * route_w, axis=1, keepdims=True)
    dchosen = (dweight - mean_term) / chosen_sum
    id_hits = (
        picked_ids[:, :, None] == jnp.arange(experts_all, dtype=jnp.int32)[None, None, :]
    ).astype(jnp.float32)
    dprobs = jnp.sum(id_hits * dchosen[:, :, None], axis=1)
    dlogits = router_probs * (dprobs - jnp.sum(router_probs * dprobs, axis=1, keepdims=True))
    router_term = jnp.dot(normed.astype(jnp.float32).T, dlogits, precision=lax.Precision.HIGHEST)
    router_grad = lax.psum(router_term, ("dp", "ctx"))
    slot_cot = jnp.einsum(
        "se,sd->ed", combine, cot_rows, preferred_element_type=jnp.float32
    ).astype(jnp.bfloat16)
    slot_cot = slot_cot.reshape(-1, local_count, capacity, model_width)
    cot_arrived = route_slots(slot_cot)
    down_term = jnp.einsum(
        "sjcf,sjcd->jfd", activated, cot_arrived, preferred_element_type=jnp.float32
    )
    dact = jnp.einsum("sjcd,jfd->sjcf", cot_arrived, down_local, preferred_element_type=jnp.float32)
    sigmoid_gate = jax.nn.sigmoid(gate_pre)
    dgate = (dact * up_pre * sigmoid_gate * (1.0 + gate_pre * (1.0 - sigmoid_gate))).astype(
        jnp.bfloat16
    )
    dup = (dact * gate_pre * sigmoid_gate).astype(jnp.bfloat16)
    gate_term = jnp.einsum("sjcd,sjcf->jdf", arrived, dgate, preferred_element_type=jnp.float32)
    up_term = jnp.einsum("sjcd,sjcf->jdf", arrived, dup, preferred_element_type=jnp.float32)
    gate_out, up_out = in_one_piece(
        (gate_term.astype(jnp.bfloat16), up_term.astype(jnp.bfloat16)), "dp", 1, 0, 2
    )
    down_out = lax.all_to_all(
        down_term.astype(jnp.bfloat16), "dp", split_axis=2, concat_axis=0, tiled=True
    )
    return (layer_out[None], router_grad, gate_out, up_out, down_out)


def solution(mesh):
    placed = (
        P("dp", "ctx", None),
        P("dp", "ctx", "exp", None),
        P("exp", None),
        P(),
        P("exp", None, None),
        P("exp", None),
        P(),
        P(),
        P("dp", "ctx", None),
        P("dp", "ctx"),
        P("ctx", None, "exp"),
        P("ctx", None, "exp"),
        P("ctx", "exp", None),
        P("dp", "ctx", None),
    )
    return jax.shard_map(
        local,
        mesh=mesh,
        in_specs=placed,
        out_specs=(
            P("dp", "ctx", None),
            P(),
            P("ctx", "dp", "exp"),
            P("ctx", "dp", "exp"),
            P("ctx", "exp", "dp"),
        ),
        check_vma=False,
    )
```

profile of v0, /device:TPU:88, one launch (start us, length us, event | category | flops | bytes accessed | tf_op | source)
XLA Modules:
  0.0 998.6 jit_solution(10595866600486797685)
XLA Ops:
  10.4 5.8 all-to-all-start
  16.3 29.8 %all-to-all-done = f32[8,128,576]{1,2,0:T(8,128)} async-done(((f32[8,128,576]{1,2,0:T(8,128)}), f32[8,128,576]{1,2,0:T(8,128)}, u32[]{:S(2)}, u32[]{:S(2)}) %all-to-all-start) | async-done | bytes 2359328 | tf_op jit(solution)/shard_map/all_to_all | solution.py:15
  49.0 37.8 %all-gather = s32[1,2048]{1,0:T(1,128)S(1)} all-gather(s32[1,128]{1,0:T(1,128)S(1)} %copy-done.4), channel_id=2, replica_groups=mesh['dp'=2,'ctx'=16,'exp'=8] {'ctx'}, dimensions={1}, use_global_device_ids=true | all-gather | bytes 8704 | tf_op jit(solution)/shard_map/all_gather | solution.py:95
  87.1 26.5 %all-gather.3.cloned.1.call-done = bf16[2048,576]{0,1:T(8,128)(2,1)} async-done(((bf16[128,576]{0,1:T(8,128)(2,1)}), bf16[2048,576]{0,1:T(8,128)(2,1)}) %all-gather.3.cloned.1.call-update) | async-done | bytes 2359312 | tf_op jit(solution)/shard_map/all_gather | solution.py:94
  126.0 83.0 %all-reduce.4.cloned.1.call-done = f32[128,2560]{1,0:T(8,128)} async-done(((f32[128,2560]{1,0:T(8,128)}), f32[128,2560]{1,0:T(8,128)}) %all-reduce.4.cloned.1.call-update) | async-done | bytes 1310736 | tf_op jit(solution)/shard_map/psum | solution.py:126
  210.8 3.9 convolution_convert_fusion.2
  214.7 8.9 all-to-all-start.1
  223.7 113.3 %all-to-all-done.1 = bf16[32,1,32,2560]{3,2,1,0:T(8,128)(2,1)} async-done(((bf16[32,1,32,2560]{3,2,1,0:T(8,128)(2,1)}), bf16[32,1,32,2560]{3,2,1,0:T(8,128)(2,1)}, u32[]{:S(2)}, u32[]{:S(2)}) %all-to-all-start.1) | async-done | bytes 5242912 | tf_op jit(solution)/shard_map/all_to_all | solution.py:58
  336.9 4.4 fusion.55
  341.4 5.4 multiply_convert_fusion.2
  351.4 12.1 %all-to-all-start.2 = ((bf16[32,1,32,2560]{3,2,1,0:T(8,128)(2,1)}), bf16[32,1,32,2560]{3,2,1,0:T(8,128)(2,1)}, u32[]{:S(2)}, u32[]{:S(2)}) async-start(bf16[32,1,32,2560]{3,2,1,0:T(8,128)(2,1)} %fusion.13), calls=%async_computation.2 | async-start | bytes 10485760 | tf_op jit(solution)/shard_map/all_to_all | solution.py:179
  364.6 5.1 gather_fusion
  370.0 107.0 %all-to-all-done.2 = bf16[32,1,32,2560]{3,2,1,0:T(8,128)(2,1)} async-done(((bf16[32,1,32,2560]{3,2,1,0:T(8,128)(2,1)}), bf16[32,1,32,2560]{3,2,1,0:T(8,128)(2,1)}, u32[]{:S(2)}, u32[]{:S(2)}) %all-to-all-start.2) | async-done | bytes 5242912 | tf_op jit(solution)/shard_map/all_to_all | solution.py:179
  477.0 4.1 convolution_bitcast_fusion
  481.1 5.1 gather_fusion.1
  486.4 23.5 %psum.30 = f32[128,6]{0,1:T(8,128)S(1)} all-reduce(f32[128,6]{0,1:T(8,128)S(1)} %and_select_fusion), channel_id=1, replica_groups=mesh['dp'=2,'ctx'=16,'exp'=8] {'exp'}, use_global_device_ids=true, to_apply=%region_15.16 | all-reduce | flops 768 | bytes 6144 | tf_op jit(solution)/shard_map/psum | solution.py:185
  510.4 5.0 convolution_convert_fusion
  515.4 9.6 all-to-all-start.3
  525.0 4.4 fusion.159
  530.9 158.4 %all-reduce.6.cloned.1.call-done = f32[128,2560]{1,0:T(8,128)} async-done(((f32[128,2560]{1,0:T(8,128)}), f32[128,2560]{1,0:T(8,128)}) %all-reduce.6.cloned.1.call-update) | async-done | bytes 1310736 | tf_op jit(solution)/shard_map/psum | solution.py:185
  691.6 4.1 fusion.61
  695.8 3.9 fusion.38
  704.9 8.9 copy.117
  714.4 18.2 %reduce.3 = bf16[2560,384]{1,0:T(8,128)(2,1)} reduce(bf16[2560,1,384]{2,1,0:T(2,128)(2,1)} %bitcast.237, bf16[]{:T(256)} %broadcast.489), dimensions={1}, to_apply=%bitcast.212.reduce_sub_computation | reduce | bytes 3932162
  735.3 8.4 all_to_all.50
  743.7 4.2 reshape.426
  750.5 4.7 fusion.32
  760.5 6.3 copy.118
  766.8 15.4 %reduce.4 = bf16[2560,192]{1,0:T(8,128)(2,1)S(1)} reduce(bf16[2560,1,192]{2,1,0:T(2,128)(2,1)} %bitcast.241, bf16[]{:T(256)} %broadcast.489), dimensions={1}, to_apply=%bitcast.214.reduce_sub_computation | reduce | bytes 1966082
  784.5 5.6 all_to_all.51
  793.0 5.1 copy.119
  801.5 188.8 %all-reduce.8.cloned.1.call-done = f32[2560,32]{0,1:T(8,128)} async-done(((f32[2560,32]{0,1:T(8,128)}), f32[2560,32]{0,1:T(8,128)}) %all-reduce.8.cloned.1.call-update) | async-done | bytes 327696 | tf_op jit(solution)/shard_map/psum | solution.py:195
  (104 shorter events, 57.5 us)
Async XLA Ops:
  7.2 340.4 %copy-start = (bf16[2,192,2560]{2,1,0:T(8,128)(2,1)S(1)}, bf16[2,192,2560]{2,1,0:T(8,128)(2,1)}, u32[]{:S(2)}) copy-start(bf16[2,192,2560]{2,1,0:T(8,128)(2,1)} %param.26) | copy-start | bytes 5898244
  10.4 5.9 copy-start.5
  10.4 35.7 %all-to-all-start = ((f32[8,128,576]{1,2,0:T(8,128)}), f32[8,128,576]{1,2,0:T(8,128)}, u32[]{:S(2)}, u32[]{:S(2)}) async-start(f32[8,128,576]{1,2,0:T(8,128)} %broadcast_in_dim.34), calls=%async_computation | async-start | bytes 4718592 | tf_op jit(solution)/shard_map/all_to_all | solution.py:15
  16.1 32.8 %copy-start.4 = (s32[1,128]{1,0:T(1,128)S(1)}, s32[1,128]{1,0:T(1,128)}, u32[]{:S(2)}) copy-start(s32[1,128]{1,0:T(1,128)} %param.23) | copy-start | bytes 1540
  16.2 97.5 %copy-start.7 = (bf16[1,128,2,576]{1,3,2,0:T(8,128)(2,1)S(1)}, bf16[1,128,2,576]{1,3,2,0:T(8,128)(2,1)}, u32[]{:S(2)}) copy-start(bf16[1,128,2,576]{1,3,2,0:T(8,128)(2,1)} %param.15) | copy-start | bytes 884740
  16.2 97.4 %all-gather.3.cloned.1.call-start = ((), (), s32[]{:S(2)}) async-start(), calls=%async_computation.6 | async-start | bytes 2506752 | tf_op jit(solution)/shard_map/all_gather | solution.py:94
  48.9 160.1 %all-reduce.4.cloned.1.call-start = ((), (), s32[]{:S(2)}) async-start(), calls=%async_computation.7 | async-start | bytes 2621440 | tf_op jit(solution)/shard_map/psum | solution.py:126
  118.3 2.9 copy-start.1
  121.2 1.5 copy-start.2
  121.2 4.3 copy-start.3
  214.7 122.2 %all-to-all-start.1 = ((bf16[32,1,32,2560]{3,2,1,0:T(8,128)(2,1)}), bf16[32,1,32,2560]{3,2,1,0:T(8,128)(2,1)}, u32[]{:S(2)}, u32[]{:S(2)}) async-start(bf16[32,1,32,2560]{3,2,1,0:T(8,128)(2,1)} %bitcast.235), calls=%async_computation.1 | async-start | bytes 10485760 | tf_op jit(solution)/shard_map/all_to_all | solution.py:58
  336.9 4.5 copy-start.6
  341.4 5.4 copy-start.9
  346.8 0.8 copy-start.12
  351.4 12.7 %copy-start.8 = (bf16[2560,32]{0,1:T(8,128)(2,1)S(1)}, bf16[2560,32]{0,1:T(8,128)(2,1)}, u32[]{:S(2)}) copy-start(bf16[2560,32]{0,1:T(8,128)(2,1)} %param.21) | copy-start | bytes 491524
  351.4 125.5 %all-to-all-start.2 = ((bf16[32,1,32,2560]{3,2,1,0:T(8,128)(2,1)}), bf16[32,1,32,2560]{3,2,1,0:T(8,128)(2,1)}, u32[]{:S(2)}, u32[]{:S(2)}) async-start(bf16[32,1,32,2560]{3,2,1,0:T(8,128)(2,1)} %fusion.13), calls=%async_computation.2 | async-start | bytes 10485760 | tf_op jit(solution)/shard_map/all_to_all | solution.py:179
  515.4 176.2 %all-to-all-start.3 = ((bf16[32,1,32,2560]{3,2,1,0:T(8,128)(2,1)}), bf16[32,1,32,2560]{3,2,1,0:T(8,128)(2,1)}, u32[]{:S(2)}, u32[]{:S(2)}) async-start(bf16[32,1,32,2560]{3,2,1,0:T(8,128)(2,1)} %bitcast.236), calls=%async_computation.3 | async-start | bytes 10485760 | tf_op jit(solution)/shard_map/all_to_all | solution.py:58
  525.0 164.4 %all-reduce.6.cloned.1.call-start = ((), (), s32[]{:S(2)}) async-start(), calls=%async_computation.8 | async-start | bytes 2621440 | tf_op jit(solution)/shard_map/psum | solution.py:185
  529.4 460.9 %all-reduce.8.cloned.1.call-start = ((), (), s32[]{:S(2)}) async-start(), calls=%async_computation.9 | async-start | bytes 655360 | tf_op jit(solution)/shard_map/psum | solution.py:195
  691.6 4.1 copy-start.10
  695.8 3.9 copy-start.11
  748.0 2.5 copy-start.13
Sparse Core Ops, SparseCore 0:
  49.1 64.4 all-gather.2
  122.8 86.1 all-reduce.3
  529.6 159.7 all-reduce.5
  692.4 297.9 all-reduce.7
where the time goes:
time: 1000 us; the launch traced here: 999 us
  waiting for transfers between devices  707 us (71%)
  blocking collectives  75.3 us (8%)
  local copies, waits for them, and re-layouts  60.3 us (6%)
  matrix products  58.1 us (6%)
  other arithmetic  47.3 us (5%)
  starting transfers between devices  36.6 us (4%)
  between operations  14.2 us (1%)
    psum x1, waiting for transfers between devices, local(): router_grad = lax.psum(router_term, ('dp', 'ctx'))  189 us
    psum x1, waiting for transfers between devices, local(): moe, dweight = lax.psum((moe_part, dweight_part), 'exp')  158 us
    all_to_all x2, waiting for transfers between devices, route_slots(): lax.all_to_all(outgoing, ('dp', 'ctx'), split_axis=0, concat_axis=0, tile...  113 us
    all_to_all x1, waiting for transfers between devices, local(): lax.all_to_all(expert_part, ('dp', 'ctx'), split_axis=0, concat_axis=0, t...  107 us
    psum x1, waiting for transfers between devices, local(): attention = lax.psum(head_part, 'exp')  83 us
    all_gather x1, blocking collectives, local(): lax.all_gather(doc_ids[0], 'ctx', axis=0, tiled=True)  37.8 us
    unnamed x2, other arithmetic  33.5 us
    all_to_all x1, waiting for transfers between devices, from_everyone(): lax.all_to_all(jnp.broadcast_to(array[None], (count, *array.shape)), axis...  29.8 us
  transfers between devices with their start and end apart: 8, of which 7 were waited for; matrix products, arithmetic and copies ran while one was open for 11% of the time, Pallas kernels for 0%

commit v1 on v0

v1 whole, which is shorter than its diff:
```python
import jax
import jax.numpy as jnp
import numpy as np
from jax import lax
from jax.sharding import PartitionSpec as P

ROPE = 64
NOPE = 128
DOCS = 4
epsilon = 1e-06
BF = jnp.bfloat16
F32 = jnp.float32


def swap(array, axis):
    return lax.all_to_all(array, axis, split_axis=0, concat_axis=0, tiled=True)


def spread(array, axis):
    count = lax.axis_size(axis)
    return swap(jnp.broadcast_to(array[None], (count, *array.shape)), axis)


def partner(array, axis):
    count = lax.axis_size(axis)
    return lax.ppermute(array, axis, [(i, i ^ 1) for i in range(count)])


def rms_scale(values, gain):
    return values * lax.rsqrt(jnp.mean(values * values, axis=-1, keepdims=True) + epsilon) * gain


def rotate(rope_part, positions):
    half_width = rope_part.shape[-1] // 2
    frequency = jnp.power(
        10000.0, -2.0 * jnp.arange(half_width, dtype=F32) / rope_part.shape[-1]
    )
    angles = positions.astype(F32)[:, None] * frequency[None, :]
    cosine = jnp.cos(angles)
    sine_part = jnp.sin(angles)
    first_half = rope_part[:, :half_width]
    second = rope_part[:, half_width:]
    return jnp.concatenate(
        [first_half * cosine - second * sine_part, second * cosine + first_half * sine_part], axis=1
    )


def dot32(a, b):
    return jnp.dot(a, b, preferred_element_type=F32)


def ein32(spec, a, b):
    return jnp.einsum(spec, a, b, preferred_element_type=F32)


def local(
    tokens,
    queries,
    kv_weight,
    kv_gain,
    uv_weight,
    out_weight,
    post_gain,
    router_weight,
    expert_ids,
    doc_ids,
    gate_weight,
    up_weight,
    down_weight,
    cotangent,
):
    rows = tokens[0]
    cot_rows = cotangent[0]
    ids = expert_ids[0]
    docs = doc_ids[0]
    n_rows, width = rows.shape
    latent_width = kv_gain.shape[0]
    n_exp = lax.axis_size("exp")
    n_ctx = lax.axis_size("ctx")
    me = lax.axis_index("exp")
    col, par = me // 2, me % 2
    block = lax.axis_index("ctx")
    core = lax.axis_index("dp")
    experts = router_weight.shape[1]
    held = experts // n_ctx
    cap = 32
    quarter = held * cap // n_exp
    per = cap // quarter
    heads = queries.shape[2]

    expert_of = jnp.arange(experts, dtype=jnp.int32)
    hit = jnp.any(ids.T[None, :, :] == expert_of[:, None, None], axis=1)
    before = jnp.asarray(np.triu(np.ones((n_rows, n_rows)), 1), BF)
    rank = dot32(hit.astype(BF), before).astype(jnp.int32)
    rank = jnp.where(hit, rank, -1)
    slots = rank[:, None, :] == jnp.arange(cap, dtype=jnp.int32)[None, :, None]
    mine = rank.reshape(n_ctx, held, n_rows)
    mine = jnp.where(me // per == 0, mine[:, 0], mine[:, 1])
    pick = mine[:, None, :] == (
        (me % per) * quarter + jnp.arange(quarter, dtype=jnp.int32)[None, :, None]
    )
    pick = pick.astype(BF).reshape(n_ctx * quarter, n_rows)

    def dispatch(values):
        out = dot32(pick, values).astype(BF).reshape(n_ctx, quarter, width)
        out = swap(out, "ctx").reshape(n_ctx * quarter, width)
        return spread(out, "exp").reshape(held, per * n_ctx * quarter, width)

    share = n_rows // n_exp
    kv_rows = kv_weight.shape[0]
    columns = lax.dynamic_slice_in_dim(rows, me * kv_rows, kv_rows, 1)
    part = dot32(columns, kv_weight).reshape(n_exp, share, -1)
    compressed = jnp.sum(swap(part, "exp"), axis=0)
    positions = block * n_rows + me * share + jnp.arange(share, dtype=jnp.int32)
    latent = rms_scale(compressed[:, :latent_width], kv_gain.astype(F32)).astype(BF)
    rope_key = rotate(compressed[:, latent_width:], positions).astype(BF)
    docs_share = lax.dynamic_slice_in_dim(docs, me * share, share, 0)
    doc_of = jnp.arange(64, dtype=jnp.int32)
    doc_key = (docs_share[:, None] == doc_of[None, :]).astype(BF)
    keys = jnp.concatenate([latent, rope_key, doc_key], axis=1)
    keys = spread(spread(keys, "ctx").reshape(n_ctx * share, -1), "exp")
    keys = keys.reshape(n_exp * n_ctx * share, -1)
    key_at = np.arange(n_exp * n_ctx * share, dtype=np.int32).reshape(n_exp, n_ctx, share)
    key_at = (
        (key_at // share % n_ctx) * n_rows + (key_at // (share * n_ctx)) * share + key_at % share
    ).reshape(-1)

    cots = dispatch(cot_rows)
    down_cols = down_weight.reshape(held, -1, n_exp // 2, 2 * width // n_exp)
    down_cols = jnp.transpose(down_cols, (2, 0, 1, 3)).reshape(n_exp, -1, 2 * width // n_exp)
    down_cols = swap(down_cols, "exp")

    differs = (doc_of[None, :] < DOCS) & (docs[:, None] != doc_of[None, :])
    doc_query = jnp.where(differs, -1e30, 0.0).astype(BF)
    query = jnp.concatenate(
        [
            jnp.transpose(queries[0], (1, 0, 2)),
            jnp.broadcast_to(doc_query[None], (heads, *doc_query.shape)),
        ],
        axis=2,
    ).reshape(heads * n_rows, -1)
    query_at = block * n_rows + jnp.arange(n_rows, dtype=jnp.int32)
    score_scale = (NOPE + ROPE) ** (-0.5)
    scores = ein32("qd,kd->qk", query, keys).reshape(heads, n_rows, -1)
    reached = (jnp.asarray(key_at)[None, :] <= query_at[:, None])[None]
    scores = jnp.where(reached, scores * score_scale, -1e30)
    weights = jnp.exp(scores - jnp.max(scores, axis=-1, keepdims=True))
    total = jnp.sum(weights, axis=-1, keepdims=True)
    mixed = (ein32("hqk,kl->hql", weights.astype(BF), keys[:, :latent_width]) / total).astype(BF)
    head_values = jnp.concatenate(
        [dot32(mixed[h], uv_weight[h]).astype(BF) for h in range(heads)], axis=1
    )
    part = dot32(head_values, out_weight).astype(BF).reshape(n_exp, share, width)
    attention = jnp.sum(swap(part, "exp").astype(F32), axis=0)
    own_rows = lax.dynamic_slice_in_dim(rows, me * share, share, 0).astype(F32)
    hidden = spread((own_rows + attention).astype(BF), "exp").reshape(n_rows, width)
    normed = rms_scale(hidden.astype(F32), post_gain.astype(F32)).astype(BF)
    arrived = dispatch(normed)

    logits = lax.dot_general(
        router_weight, normed, (((0,), (1,)), ((), ())), preferred_element_type=F32
    )
    probs = jax.nn.softmax(logits, axis=0)
    chosen = jnp.where(hit, probs, 0.0)
    chosen_sum = jnp.sum(chosen, axis=0, keepdims=True)
    route_w = chosen / chosen_sum
    route_b = route_w.astype(BF)
    slot_w = jnp.sum(jnp.where(slots, route_b.astype(F32)[:, None, :], 0.0), axis=2)
    slot_w = swap(slot_w.reshape(n_ctx, held * cap), "ctx")
    slot_w = jnp.transpose(slot_w.reshape(n_ctx, held, per, quarter), (1, 2, 0, 3))
    slot_w = slot_w.reshape(held, -1, 1)

    gate_pre = ein32("jrd,jdf->jrf", arrived, gate_weight)
    up_pre = ein32("jrd,jdf->jrf", arrived, up_weight)
    sigmoid_gate = jax.nn.sigmoid(gate_pre)
    activated = (gate_pre * sigmoid_gate * up_pre).astype(BF)
    wide = swap(
        jnp.broadcast_to(activated[None], (n_exp // held, *activated.shape)).reshape(
            n_exp, *activated.shape[1:]
        ),
        "exp",
    )
    result = ein32("frk,fkc->rc", wide, down_cols).astype(BF)
    result = jnp.transpose(result.reshape(per, n_ctx, quarter, -1), (1, 0, 2, 3))
    returned = swap(result.reshape(n_ctx, cap, -1), "ctx").reshape(n_ctx * cap, -1)

    half = n_rows // 2
    wide_cols = 2 * width // n_exp
    combine = jnp.where(slots, route_b[:, None, :], jnp.zeros((), BF))
    combine = combine.reshape(n_ctx, held, cap, n_rows)
    combine = jnp.where(par == 0, combine[:, 0], combine[:, 1]).reshape(n_ctx * cap, n_rows)
    moe = lax.dot_general(
        combine, returned, (((0,), (0,)), ((), ())), preferred_element_type=F32
    )
    kept = lax.dynamic_slice_in_dim(moe, par * half, half, 0)
    sent = lax.dynamic_slice_in_dim(moe, (1 - par) * half, half, 0)
    own_hidden = lax.dynamic_slice(hidden, (par * half, col * wide_cols), (half, wide_cols))
    out = own_hidden.astype(F32) + (kept + partner(sent, "exp"))
    out = spread(out.astype(BF), "exp").reshape(n_exp // 2, 2, half, wide_cols)
    layer_out = jnp.transpose(out, (1, 2, 0, 3)).reshape(n_rows, width)

    dact = ein32("jrd,jfd->jrf", cots, down_weight)
    dweight = jnp.sum(activated.astype(F32) * dact, axis=2)
    dweight = jnp.transpose(dweight.reshape(held, per, n_ctx, quarter), (2, 0, 1, 3))
    dweight = swap(dweight.reshape(n_ctx, held * cap), "ctx")
    dweight = jnp.sum(spread(dweight, "exp"), axis=0).reshape(experts, cap, 1)
    dact = dact * slot_w
    dgate = (dact * up_pre * sigmoid_gate * (1.0 + gate_pre * (1.0 - sigmoid_gate))).astype(BF)
    dup = (dact * gate_pre * sigmoid_gate).astype(BF)
    weighted = (activated.astype(F32) * slot_w).astype(BF)
    split = width // 2
    near, far = core * split, (1 - core) * split
    cut = lambda array, at: lax.dynamic_slice_in_dim(array, at, split, 2)
    grads = []
    for left, right, spec in (
        (arrived, dgate, "jrd,jrf->jdf"),
        (arrived, dup, "jrd,jrf->jdf"),
        (cots, weighted, "jrd,jrf->jfd"),
    ):
        other = partner(ein32(spec, cut(left, far), right).astype(BF), "dp")
        grads.append((ein32(spec, cut(left, near), right) + other.astype(F32)).astype(BF))

    dweight = jnp.sum(jnp.where(slots, dweight, 0.0), axis=1)
    mean_term = jnp.sum(dweight * route_w, axis=0, keepdims=True)
    dprobs = jnp.where(hit, (dweight - mean_term) / chosen_sum, 0.0)
    dlogits = probs * (dprobs - jnp.sum(probs * dprobs, axis=0, keepdims=True))
    normed_cols = lax.dynamic_slice_in_dim(normed, me * (width // n_exp), width // n_exp, 1)
    term = jnp.dot(dlogits, normed_cols.astype(F32), precision=lax.Precision.HIGHEST)
    term = term + partner(term, "dp")
    term = jnp.sum(spread(term, "ctx"), axis=0)
    router_grad = jnp.transpose(spread(term, "exp"), (0, 2, 1)).reshape(width, experts)
    return (layer_out[None], router_grad, *grads)


def solution(mesh):
    placed = (
        P("dp", "ctx", None),
        P("dp", "ctx", "exp", None),
        P("exp", None),
        P(),
        P("exp", None, None),
        P("exp", None),
        P(),
        P(),
        P("dp", "ctx", None),
        P("dp", "ctx"),
        P("ctx", None, "exp"),
        P("ctx", None, "exp"),
        P("ctx", "exp", None),
        P("dp", "ctx", None),
    )
    return jax.shard_map(
        local,
        mesh=mesh,
        in_specs=placed,
        out_specs=(
            P("dp", "ctx", None),
            P(),
            P("ctx", "dp", "exp"),
            P("ctx", "dp", "exp"),
            P("ctx", "exp", "dp"),
        ),
        check_vma=False,
    )
```

time: 1000 us -> 468 us (0.47)
  waiting for transfers between devices: 707 us -> 167 us
  blocking collectives: 75.3 us -> 148 us
  other arithmetic: 47.3 us -> 8 us
  local copies, waits for them, and re-layouts: 60.3 us -> 22.6 us
  starting transfers between devices: 36.6 us -> 65.3 us
  between operations: 14.2 us -> 1.25 us
    psum x3 -> x0, waiting for transfers between devices: 430 us -> none  [the longest x1 189 us: local(): router_grad = lax.psum(router_term, ('dp', 'ctx'))]
    all_to_all x2 -> x6, blocking collectives: 14 us -> 148 us  [swap(): return lax.all_to_all(array, axis, split_axis=0, concat_axis=0, tiled=True)]
    all_to_all x4 -> x12, waiting for transfers between devices: 250 us -> 164 us  [swap(): return lax.all_to_all(array, axis, split_axis=0, concat_axis=0, tiled=True)]
    all_gather x1 -> x0, blocking collectives: 37.8 us -> none  [local(): lax.all_gather(doc_ids[0], 'ctx', axis=0, tiled=True)]
    unnamed x2 -> x0, other arithmetic: 33.5 us -> none
    all_gather x1 -> x0, waiting for transfers between devices: 26.5 us -> none  [local(): lax.all_gather(key_rows, 'ctx', axis=0, tiled=True)]
    all_to_all x4 -> x12, starting transfers between devices: 36.4 us -> 62.6 us  [swap(): return lax.all_to_all(array, axis, split_axis=0, concat_axis=0, tiled=True)]
    psum x1 -> x0, blocking collectives: 23.5 us -> none  [local(): moe, dweight = lax.psum((moe_part, dweight_part), 'exp')]
  transfers between devices with their start and end apart: 8 -> 17, of which waited for: 7 -> 13; matrix products, arithmetic and copies ran while one was open for 11% -> 11% of each run, Pallas kernels for 0% -> 0%
where the time goes in v1:
time: 468 us; the launch traced here: 462 us
  waiting for transfers between devices  167 us (36%)
  blocking collectives  148 us (32%)
  starting transfers between devices  65.3 us (14%)
  matrix products  49.8 us (11%)
  local copies, waits for them, and re-layouts  22.6 us (5%)
  other arithmetic  8 us (2%)
    all_to_all x12, waiting for transfers between devices, swap(): return lax.all_to_all(array, axis, split_axis=0, concat_axis=0, tiled=True)  164 us
    all_to_all x6, blocking collectives, swap(): return lax.all_to_all(array, axis, split_axis=0, concat_axis=0, tiled=True)  148 us
    all_to_all x12, starting transfers between devices, swap(): return lax.all_to_all(array, axis, split_axis=0, concat_axis=0, tiled=True)  62.6 us
    dot_general x12, matrix products, ein32(): return jnp.einsum(spec, a, b, preferred_element_type=F32)  42.4 us
    broadcast_in_dim x9, local copies, waits for them, and re-layouts, spread(): return swap(jnp.broadcast_to(array[None], (count, *array.shape)), axis)  9.6 us
  transfers between devices with their start and end apart: 17, of which 13 were waited for; matrix products, arithmetic and copies ran while one was open for 11% of the time, Pallas kernels for 0%

profile of v1, /device:TPU:88, one launch (start us, length us, event | category | flops | bytes accessed | tf_op | source)
XLA Modules:
  0.0 462.5 jit_solution(18036925274263393685)
XLA Ops:
  3.8 5.7 %all-to-all-start = ((f32[8,16,576]{2,1,0:T(8,128)}), f32[8,16,576]{2,1,0:T(8,128)S(1)}, u32[]{:S(2)}, u32[]{:S(2)}) async-start(f32[8,16,576]{2,1,0:T(8,128)} %fusion.28), calls=%async_computation | async-start | bytes 655360 | tf_op jit(solution)/shard_map/all_to_all | solution.py:16
  10.9 6.5 %all-to-all-done = f32[8,16,576]{2,1,0:T(8,128)S(1)} async-done(((f32[8,16,576]{2,1,0:T(8,128)}), f32[8,16,576]{2,1,0:T(8,128)S(1)}, u32[]{:S(2)}, u32[]{:S(2)}) %all-to-all-start) | async-done | bytes 294944 | tf_op jit(solution)/shard_map/all_to_all | solution.py:16
  17.9 18.9 %all_to_all.98 = bf16[16,16,640]{2,1,0:T(8,128)(2,1)S(1)} all-to-all(bf16[16,16,640]{2,1,0:T(8,128)(2,1)S(1)} %broadcast_in_dim.103), channel_id=1, replica_groups=mesh['dp'=2,'ctx'=16,'exp'=8] {'ctx'}, dimensions={0} | all-to-all | bytes 655360 | tf_op jit(solution)/shard_map/all_to_all | solution.py:16
  38.5 4.5 all-to-all-start.2
  43.6 30.3 %all-to-all-done.2 = bf16[8,256,640]{2,1,0:T(8,128)(2,1)} async-done(((bf16[8,256,640]{2,1,0:T(8,128)(2,1)}), bf16[8,256,640]{2,1,0:T(8,128)(2,1)}, u32[]{:S(2)}, u32[]{:S(2)}) %all-to-all-start.2) | async-done | bytes 2621472 | tf_op jit(solution)/shard_map/all_to_all | solution.py:16
  80.7 14.4 %all_to_all.99 = bf16[8,16,2560]{2,1,0:T(8,128)(2,1)S(1)} all-to-all(bf16[8,16,2560]{2,1,0:T(8,128)(2,1)S(1)} %bitcast.154), channel_id=1, replica_groups=mesh['dp'=2,'ctx'=16,'exp'=8] {'exp'}, dimensions={0} | all-to-all | bytes 1310720 | tf_op jit(solution)/shard_map/all_to_all | solution.py:16
  97.0 3.5 all-to-all-start.4
  102.0 9.1 %all-to-all-done.4 = bf16[8,16,2560]{2,1,0:T(8,128)(2,1)S(1)} async-done(((bf16[8,16,2560]{2,1,0:T(8,128)(2,1)}), bf16[8,16,2560]{2,1,0:T(8,128)(2,1)S(1)}, u32[]{:S(2)}, u32[]{:S(2)}) %all-to-all-start.4) | async-done | bytes 655392 | tf_op jit(solution)/shard_map/all_to_all | solution.py:16
  111.1 7.3 %all-to-all-start.11 = ((bf16[16,8,2560]{2,1,0:T(8,128)(2,1)}), bf16[16,8,2560]{2,1,0:T(8,128)(2,1)}, u32[]{:S(2)}, u32[]{:S(2)}) async-start(bf16[16,8,2560]{2,1,0:T(8,128)(2,1)} %fusion.1), calls=%async_computation.11 | async-start | bytes 1310720 | tf_op jit(solution)/shard_map/all_to_all | solution.py:16
  119.3 15.7 %all-to-all-done.11 = bf16[16,8,2560]{2,1,0:T(8,128)(2,1)} async-done(((bf16[16,8,2560]{2,1,0:T(8,128)(2,1)}), bf16[16,8,2560]{2,1,0:T(8,128)(2,1)}, u32[]{:S(2)}, u32[]{:S(2)}) %all-to-all-start.11) | async-done | bytes 655392 | tf_op jit(solution)/shard_map/all_to_all | solution.py:16
  135.0 21.7 %all_to_all.100 = bf16[16,8,2560]{2,1,0:T(8,128)(2,1)S(1)} all-to-all(bf16[16,8,2560]{2,1,0:T(8,128)(2,1)S(1)} %fusion), channel_id=1, replica_groups=mesh['dp'=2,'ctx'=16,'exp'=8] {'ctx'}, dimensions={0} | all-to-all | bytes 1310720 | tf_op jit(solution)/shard_map/all_to_all | solution.py:16
  157.1 63.0 %all_to_all.101 = bf16[8,128,2560]{2,1,0:T(8,128)(2,1)} all-to-all(bf16[8,128,2560]{2,1,0:T(8,128)(2,1)S(1)} %broadcast_in_dim.184), channel_id=1, replica_groups=mesh['dp'=2,'ctx'=16,'exp'=8] {'exp'}, dimensions={0} | all-to-all | bytes 10485760 | tf_op jit(solution)/shard_map/all_to_all | solution.py:16
  220.1 3.9 broadcast_in_dim.188
  224.0 4.7 %all-to-all-start.12 = ((bf16[8,128,2560]{2,1,0:T(8,128)(2,1)}), bf16[8,128,2560]{2,1,0:T(8,128)(2,1)}, u32[]{:S(2)}, u32[]{:S(2)}) async-start(bf16[8,128,2560]{2,1,0:T(8,128)(2,1)} %broadcast_in_dim.188), calls=%async_computation.12 | async-start | bytes 10485760 | tf_op jit(solution)/shard_map/all_to_all | solution.py:16
  228.7 5.4 %fusion.101 = f32[2,512,192]{1,2,0:T(8,128)} fusion(bf16[2,512,2560]{2,1,0:T(8,128)(2,1)} %bitcast.144, bf16[2,2560,192]{1,2,0:T(8,128)(2,1)S(1)} %copy-done), kind=kOutput, calls=%fused_computation.153 | convolution fusion | flops 1006632960 | bytes 7995392 | tf_op jit(solution)/shard_map/jrd,jdf->jrf/dot_general | solution.py:53
  235.9 49.8 %all-to-all-done.12 = bf16[8,128,2560]{2,1,0:T(8,128)(2,1)} async-done(((bf16[8,128,2560]{2,1,0:T(8,128)(2,1)}), bf16[8,128,2560]{2,1,0:T(8,128)(2,1)}, u32[]{:S(2)}, u32[]{:S(2)}) %all-to-all-start.12) | async-done | bytes 5242912 | tf_op jit(solution)/shard_map/all_to_all | solution.py:16
  285.7 5.9 %fusion.24 = (f32[2,512]{1,0:T(2,128)S(1)}, bf16[2,512,192]{1,2,0:T(8,128)(2,1)S(1)}, f32[2,512,192]{1,2,0:T(8,128)}) fusion(f32[2,512,192]{1,2,0:T(8,128)S(1)} %fusion.102, f32[2,512,192]{1,2,0:T(8,128)S(1)} %copy-done.3, bf16[2,512,2560]{2,1,0:T(8,128)(2,1)} %bitcast.42, bf16[2,192,2560]{2,1,0:T(8,128)(2,1)} %param.28), kind=kOutput, calls=%fused_computation.47 | convolution fusion | flops 1008401408 | bytes 9965568 | tf_op jit(solution)/shard_map/jrd,jfd->jrf/dot_general | solution.py:53
  291.8 17.6 %all_to_all.102 = f32[16,1,64]{2,1,0:T(1,128)S(1)} all-to-all(f32[16,1,64]{2,1,0:T(1,128)S(1)} %copy.74), channel_id=1, replica_groups=mesh['dp'=2,'ctx'=16,'exp'=8] {'ctx'}, dimensions={0} | all-to-all | bytes 8192 | tf_op jit(solution)/shard_map/all_to_all | solution.py:16
  319.6 3.9 all-to-all-start.8
  327.0 18.9 %all-to-all-done.8 = bf16[8,192,640]{2,1,0:T(8,128)(2,1)S(1)} async-done(((bf16[8,192,640]{2,1,0:T(8,128)(2,1)}), bf16[8,192,640]{2,1,0:T(8,128)(2,1)S(1)}, u32[]{:S(2)}, u32[]{:S(2)}) %all-to-all-start.8) | async-done | bytes 1966112 | tf_op jit(solution)/shard_map/all_to_all | solution.py:16
  345.8 12.5 %all_to_all.103 = f32[16,1,64]{2,1,0:T(1,128)S(1)} all-to-all(f32[16,1,64]{2,1,0:T(1,128)S(1)} %bitcast.170), channel_id=1, replica_groups=mesh['dp'=2,'ctx'=16,'exp'=8] {'ctx'}, dimensions={0} | all-to-all | bytes 8192 | tf_op jit(solution)/shard_map/all_to_all | solution.py:16
  359.7 4.3 all-to-all-start.7
  366.6 14.6 %all-to-all-done.7 = bf16[8,512,192]{1,2,0:T(8,128)(2,1)} async-done(((bf16[8,512,192]{1,2,0:T(8,128)(2,1)}), bf16[8,512,192]{1,2,0:T(8,128)(2,1)}, u32[]{:S(2)}, u32[]{:S(2)}) %all-to-all-start.7) | async-done | bytes 1572896 | tf_op jit(solution)/shard_map/all_to_all | solution.py:16
  382.2 7.9 %all-to-all-start.15 = ((f32[16,32,320]{2,1,0:T(8,128)}), f32[16,32,320]{2,1,0:T(8,128)}, u32[]{:S(2)}, u32[]{:S(2)}) async-start(f32[16,32,320]{2,1,0:T(8,128)} %broadcast_in_dim.194), calls=%async_computation.15 | async-start | bytes 1572864 | tf_op jit(solution)/shard_map/all_to_all | solution.py:16
  393.8 12.3 %all-to-all-done.15 = f32[16,32,320]{2,1,0:T(8,128)} async-done(((f32[16,32,320]{2,1,0:T(8,128)}), f32[16,32,320]{2,1,0:T(8,128)}, u32[]{:S(2)}, u32[]{:S(2)}) %all-to-all-start.15) | async-done | bytes 655392 | tf_op jit(solution)/shard_map/all_to_all | solution.py:16
  406.1 6.9 %all-to-all-start.9 = ((bf16[16,32,640]{2,1,0:T(8,128)(2,1)}), bf16[16,32,640]{2,1,0:T(8,128)(2,1)}, u32[]{:S(2)}, u32[]{:S(2)}) async-start(bf16[16,32,640]{2,1,0:T(8,128)(2,1)} %bitcast.142), calls=%async_computation.9 | async-start | bytes 1310720 | tf_op jit(solution)/shard_map/all_to_all | solution.py:16
  415.2 3.4 convolution_convert_fusion.3
  427.7 6.5 %all-to-all-start.16 = ((f32[8,32,320]{2,1,0:T(8,128)}), f32[8,32,320]{2,1,0:T(8,128)S(1)}, u32[]{:S(2)}, u32[]{:S(2)}) async-start(f32[8,32,320]{2,1,0:T(8,128)} %broadcast_in_dim.195), calls=%async_computation.16 | async-start | bytes 786432 | tf_op jit(solution)/shard_map/all_to_all | solution.py:16
  444.7 4.0 all-to-all-start.10
  448.7 3.6 add_convert_fusion.1
  452.4 3.6 add_convert_fusion.2
  456.0 3.8 add_convert_fusion
  (140 shorter events, 67.3 us)
Async XLA Ops:
  0.6 228.0 %copy-start = (bf16[2,2560,192]{1,2,0:T(8,128)(2,1)S(1)}, bf16[2,2560,192]{1,2,0:T(8,128)(2,1)}, u32[]{:S(2)}) copy-start(bf16[2,2560,192]{1,2,0:T(8,128)(2,1)} %param.26) | copy-start | bytes 5898244
  3.8 13.6 %all-to-all-start = ((f32[8,16,576]{2,1,0:T(8,128)}), f32[8,16,576]{2,1,0:T(8,128)S(1)}, u32[]{:S(2)}, u32[]{:S(2)}) async-start(f32[8,16,576]{2,1,0:T(8,128)} %fusion.28), calls=%async_computation | async-start | bytes 655360 | tf_op jit(solution)/shard_map/all_to_all | solution.py:16
  38.5 4.5 copy-start.10
  38.5 4.8 %copy-start.16 = (s32[1,128]{1,0:T(1,128)S(1)}, s32[1,128]{1,0:T(1,128)}, u32[]{:S(2)}) copy-start(s32[1,128]{1,0:T(1,128)} %param.25) | copy-start | bytes 1540
  38.5 4.9 %copy-start.13 = (s32[2048]{0:T(1024)S(1)}, s32[2048]{0:T(1024)}, u32[]{:S(2)}) copy-start(s32[2048]{0:T(1024)} %constant.115.clone) | copy-start | bytes 24580
  38.5 35.4 %all-to-all-start.2 = ((bf16[8,256,640]{2,1,0:T(8,128)(2,1)}), bf16[8,256,640]{2,1,0:T(8,128)(2,1)}, u32[]{:S(2)}, u32[]{:S(2)}) async-start(bf16[8,256,640]{2,1,0:T(8,128)(2,1)} %broadcast_in_dim.105), calls=%async_computation.2 | async-start | bytes 5242880 | tf_op jit(solution)/shard_map/all_to_all | solution.py:16
  80.7 19.9 %copy-start.14 = (bf16[2560]{0:T(1024)(128)(2,1)S(1)}, bf16[2560]{0:T(1024)(128)(2,1)}, u32[]{:S(2)}) copy-start(bf16[2560]{0:T(1024)(128)(2,1)} %param.22) | copy-start | bytes 15364
  80.7 19.9 %copy-start.15 = (s32[1,128,6]{1,0,2:T(1,128)S(1)}, s32[1,128,6]{1,0,2:T(1,128)}, u32[]{:S(2)}) copy-start(s32[1,128,6]{1,0,2:T(1,128)} %param.24) | copy-start | bytes 9220
  80.7 19.9 %copy-start.12 = (bf16[128,128]{1,0:T(8,128)(2,1)S(1)}, bf16[128,128]{1,0:T(8,128)(2,1)}, u32[]{:S(2)}) copy-start(bf16[128,128]{1,0:T(8,128)(2,1)} %constant.114.clone) | copy-start | bytes 98308
  80.7 20.1 %copy-start.9 = (bf16[1,128,2560]{2,1,0:T(8,128)(2,1)S(1)}, bf16[1,128,2560]{2,1,0:T(8,128)(2,1)}, u32[]{:S(2)}) copy-start(bf16[1,128,2560]{2,1,0:T(8,128)(2,1)} %param.29) | copy-start | bytes 1966084
  97.0 14.1 %all-to-all-start.4 = ((bf16[8,16,2560]{2,1,0:T(8,128)(2,1)}), bf16[8,16,2560]{2,1,0:T(8,128)(2,1)S(1)}, u32[]{:S(2)}, u32[]{:S(2)}) async-start(bf16[8,16,2560]{2,1,0:T(8,128)(2,1)} %broadcast_in_dim.108), calls=%async_computation.4 | async-start | bytes 1310720 | tf_op jit(solution)/shard_map/all_to_all | solution.py:16
  111.1 23.9 %all-to-all-start.11 = ((bf16[16,8,2560]{2,1,0:T(8,128)(2,1)}), bf16[16,8,2560]{2,1,0:T(8,128)(2,1)}, u32[]{:S(2)}, u32[]{:S(2)}) async-start(bf16[16,8,2560]{2,1,0:T(8,128)(2,1)} %fusion.1), calls=%async_computation.11 | async-start | bytes 1310720 | tf_op jit(solution)/shard_map/all_to_all | solution.py:16
  224.0 61.7 %all-to-all-start.12 = ((bf16[8,128,2560]{2,1,0:T(8,128)(2,1)}), bf16[8,128,2560]{2,1,0:T(8,128)(2,1)}, u32[]{:S(2)}, u32[]{:S(2)}) async-start(bf16[8,128,2560]{2,1,0:T(8,128)(2,1)} %broadcast_in_dim.188), calls=%async_computation.12 | async-start | bytes 10485760 | tf_op jit(solution)/shard_map/all_to_all | solution.py:16
  228.7 5.4 %copy-start.2 = (bf16[8,128,2560]{2,1,0:T(8,128)(2,1)S(1)}, bf16[8,128,2560]{2,1,0:T(8,128)(2,1)}, u32[]{:S(2)}) copy-start(bf16[8,128,2560]{2,1,0:T(8,128)(2,1)} %all_to_all.101) | copy-start | bytes 15728644
  228.7 5.4 %copy-start.7 = (bf16[2,2560,192]{1,2,0:T(8,128)(2,1)S(1)}, bf16[2,2560,192]{1,2,0:T(8,128)(2,1)}, u32[]{:S(2)}) copy-start(bf16[2,2560,192]{1,2,0:T(8,128)(2,1)} %param.27) | copy-start | bytes 5898244
  234.1 51.6 %copy-start.3 = (f32[2,512,192]{1,2,0:T(8,128)S(1)}, f32[2,512,192]{1,2,0:T(8,128)}, u32[]{:S(2)}) copy-start(f32[2,512,192]{1,2,0:T(8,128)} %fusion.101) | copy-start | bytes 2359300
  235.9 55.6 %copy-start.5 = (f32[2,512,192]{1,2,0:T(8,128)}, f32[2,512,192]{1,2,0:T(8,128)S(1)}, u32[]{:S(2)}) copy-start(f32[2,512,192]{1,2,0:T(8,128)S(1)} %fusion.102) | copy-start | bytes 2359300
  310.0 9.5 %all-to-all-start.14 = ((f32[8,1,1024]{2,1,0:T(1,128)}), f32[8,1,1024]{2,1,0:T(1,128)S(1)}, u32[]{:S(2)}, u32[]{:S(2)}) async-start(f32[8,1,1024]{2,1,0:T(1,128)} %reshape.319), calls=%async_computation.14 | async-start | bytes 65536 | tf_op jit(solution)/shard_map/all_to_all | solution.py:16
  319.6 5.1 %copy-start.11 = (bf16[2560,32]{0,1:T(8,128)(2,1)S(1)}, bf16[2560,32]{0,1:T(8,128)(2,1)}, u32[]{:S(2)}) copy-start(bf16[2560,32]{0,1:T(8,128)(2,1)} %param.23) | copy-start | bytes 491524
  319.6 26.2 %all-to-all-start.8 = ((bf16[8,192,640]{2,1,0:T(8,128)(2,1)}), bf16[8,192,640]{2,1,0:T(8,128)(2,1)S(1)}, u32[]{:S(2)}, u32[]{:S(2)}) async-start(bf16[8,192,640]{2,1,0:T(8,128)(2,1)} %bitcast.151), calls=%async_computation.8 | async-start | bytes 3932160 | tf_op jit(solution)/shard_map/all_to_all | solution.py:16
  359.7 21.5 %all-to-all-start.7 = ((bf16[8,512,192]{1,2,0:T(8,128)(2,1)}), bf16[8,512,192]{1,2,0:T(8,128)(2,1)}, u32[]{:S(2)}, u32[]{:S(2)}) async-start(bf16[8,512,192]{1,2,0:T(8,128)(2,1)} %bitcast.152), calls=%async_computation.7 | async-start | bytes 3145728 | tf_op jit(solution)/shard_map/all_to_all | solution.py:16
  365.3 1.3 collective-permute-start.1
  382.2 23.9 %all-to-all-start.15 = ((f32[16,32,320]{2,1,0:T(8,128)}), f32[16,32,320]{2,1,0:T(8,128)}, u32[]{:S(2)}, u32[]{:S(2)}) async-start(f32[16,32,320]{2,1,0:T(8,128)} %broadcast_in_dim.194), calls=%async_computation.15 | async-start | bytes 1572864 | tf_op jit(solution)/shard_map/all_to_all | solution.py:16
  392.9 20.5 %copy-start.4 = (f32[2,512,192]{1,2,0:T(8,128)S(1)}, f32[2,512,192]{1,2,0:T(8,128)}, u32[]{:S(2)}) copy-start(f32[2,512,192]{1,2,0:T(8,128)} %fusion.101) | copy-start | bytes 2359300
  406.1 20.8 %all-to-all-start.9 = ((bf16[16,32,640]{2,1,0:T(8,128)(2,1)}), bf16[16,32,640]{2,1,0:T(8,128)(2,1)}, u32[]{:S(2)}, u32[]{:S(2)}) async-start(bf16[16,32,640]{2,1,0:T(8,128)(2,1)} %bitcast.142), calls=%async_computation.9 | async-start | bytes 1310720 | tf_op jit(solution)/shard_map/all_to_all | solution.py:16
  418.6 30.2 %collective-permute-start.3 = (bf16[2,1280,192]{1,2,0:T(8,128)(2,1)}, bf16[2,1280,192]{1,2,0:T(8,128)(2,1)}, u32[]{:S(2)}, u32[]{:S(2)}) collective-permute-start(bf16[2,1280,192]{1,2,0:T(8,128)(2,1)} %convolution_convert_fusion.3), channel_id=1, source_target_pairs={{0,128},{128,0},{1,129},{129,1},{2,130},{130,2},{3,131},{131,3},{4... | collective-permute-start | bytes 2949128 | tf_op jit(solution)/shard_map/ppermute | solution.py:26
  422.0 30.4 %collective-permute-start.2 = (bf16[2,1280,192]{1,2,0:T(8,128)(2,1)}, bf16[2,1280,192]{1,2,0:T(8,128)(2,1)}, u32[]{:S(2)}, u32[]{:S(2)}) collective-permute-start(bf16[2,1280,192]{1,2,0:T(8,128)(2,1)} %convolution_convert_fusion.4), channel_id=1, source_target_pairs={{0,128},{128,0},{1,129},{129,1},{2,130},{130,2},{3,131},{131,3},{4... | collective-permute-start | bytes 2949128 | tf_op jit(solution)/shard_map/ppermute | solution.py:26
  427.7 16.2 %all-to-all-start.16 = ((f32[8,32,320]{2,1,0:T(8,128)}), f32[8,32,320]{2,1,0:T(8,128)S(1)}, u32[]{:S(2)}, u32[]{:S(2)}) async-start(f32[8,32,320]{2,1,0:T(8,128)} %broadcast_in_dim.195), calls=%async_computation.16 | async-start | bytes 786432 | tf_op jit(solution)/shard_map/all_to_all | solution.py:16
  435.6 7.9 %collective-permute-start = (f32[64,640]{1,0:T(8,128)S(1)}, f32[64,640]{1,0:T(8,128)S(1)}, u32[]{:S(2)}, u32[]{:S(2)}) collective-permute-start(f32[64,640]{1,0:T(8,128)S(1)} %constant_dynamic-slice_fusion), channel_id=1, source_target_pairs={{0,1},{1,0},{2,3},{3,2},{4,5},{5,4},{6,7},{7,6},{8,9},{9,8},{10,11... | collective-permute-start | bytes 491528 | tf_op jit(solution)/shard_map/ppermute | solution.py:26
  441.1 14.9 %collective-permute-start.4 = (bf16[2,192,1280]{2,1,0:T(8,128)(2,1)}, bf16[2,192,1280]{2,1,0:T(8,128)(2,1)}, u32[]{:S(2)}, u32[]{:S(2)}) collective-permute-start(bf16[2,192,1280]{2,1,0:T(8,128)(2,1)} %convolution_convert_fusion.5), channel_id=1, source_target_pairs={{0,128},{128,0},{1,129},{129,1},{2,130},{130,2},{3,131},{131,3},{4... | collective-permute-start | bytes 2949128 | tf_op jit(solution)/shard_map/ppermute | solution.py:26
  444.7 16.1 %all-to-all-start.10 = ((bf16[8,64,640]{2,1,0:T(8,128)(2,1)}), bf16[8,64,640]{2,1,0:T(8,128)(2,1)S(1)}, u32[]{:S(2)}, u32[]{:S(2)}) async-start(bf16[8,64,640]{2,1,0:T(8,128)(2,1)} %broadcast_in_dim.186), calls=%async_computation.10 | async-start | bytes 1310720 | tf_op jit(solution)/shard_map/all_to_all | solution.py:16
  456.0 6.5 %copy-start.1 = (bf16[2,2560,192]{1,2,0:T(8,128)(2,1)S(1)}, bf16[2,2560,192]{1,2,0:T(8,128)(2,1)}, u32[]{:S(2)}) copy-start(bf16[2,2560,192]{1,2,0:T(8,128)(2,1)} %param.26) | copy-start | bytes 5898244
  (3 other events, 6.3 us)
